TPU v7x, 32 devices: a whole 2x2x4 slice. The times are simulated.
32 devices in a mesh: tiles: 8 (over z, y), freq: 4 (over x, core).
Axes of the slice: x: 2, y: 2, z: 4, core: 2. Of those that a mesh axis runs over, the one named last changes fastest.
Arguments:
- model_in: bfloat16 [4, 1024, 128], P('freq', 'tiles'), may hold values from -6 to 6
- observed: bfloat16 [4, 1024, 128], P('freq', 'tiles'), may hold values from -6 to 6
- right_factors: bfloat16 [4, 8, 2, 256, 128], P('freq', 'tiles'), may hold values from -0.375 to 0.375
- left_factors: bfloat16 [4, 8, 2, 256, 128], P('freq', 'tiles'), may hold values from -0.25 to 0.25
- tile_map: int32 [8, 2], P('tiles'), may hold values from 0 to 3, as said below
- tile_ranks: int32 [4, 8, 2], P('freq', 'tiles'), may hold values from 1 to 64
- window_mix: float32 [4, 4], replicated, may hold values from 0.1 to 0.6
Outputs:
- residual: float32 [4, 1024, 128], P('freq', 'tiles')
- gradient: float32 [4, 1024, 128], P('freq', 'tiles')
Inputs may be any that keep to these rules, and one draw needn't show every extreme that they name: `tile_map`: devices 2j and 2j+1 of tiles together list every tile row 0 to 3 exactly once, 2 distinct rows each. `tile_ranks`: the rank of the tile named by tile_map in the same slot.
All inputs are finite; a program needn't handle non-finite values.
Results may differ from a plain program's by a relative error of at most 0.0042.
Values may be sent and summed in bfloat16 or wider, within the bound.
A program may use at most 64 MiB of HBM per device.

v0:
```python
import jax
import jax.numpy as jnp
from jax import lax
from jax.sharding import PartitionSpec as P


def from_partner(value, axis, apart):
    mask = 2**apart
    pairs = [(source, source ^ mask) for source in range(lax.axis_size(axis))]
    return lax.ppermute(value, axis, pairs)


def conjugate_apply(factor, values):
    product = jnp.einsum("tar,as->trs", factor, values, preferred_element_type=jnp.float32)
    rank_width = factor.shape[2] // 2
    half_cols = values.shape[1] // 2
    real_part = product[:, :rank_width, :half_cols] + product[:, rank_width:, half_cols:]
    imag_part = product[:, :rank_width, half_cols:] - product[:, rank_width:, :half_cols]
    return jnp.concatenate([real_part, imag_part], axis=2)


def factor_apply(factor, coeffs):
    half_cols = coeffs.shape[2] // 2
    real_part = coeffs[:, :, :half_cols]
    imag_part = coeffs[:, :, half_cols:]
    upper_rows = jnp.concatenate([real_part, imag_part], axis=2)
    lower_rows = jnp.concatenate([-imag_part, real_part], axis=2)
    stacked = jnp.concatenate([upper_rows, lower_rows], axis=1)
    return jnp.einsum("tar,trs->as", factor, stacked, preferred_element_type=jnp.float32)


def rank_mask(ranks, rank_width):
    levels = lax.broadcasted_iota(jnp.int32, (ranks.shape[0], rank_width, 1), 1)
    return levels < ranks[:, None, None]


def ordered(parity, mine, theirs):
    first_order = jnp.concatenate([mine, theirs], axis=0)
    second = jnp.concatenate([theirs, mine], axis=0)
    return jnp.where(parity == 0, first_order, second)


def window_step(mixing, freq_index, rows_pred, rows_data):
    weights_row = lax.dynamic_index_in_dim(mixing, freq_index, 0, keepdims=False)
    weights_col = lax.dynamic_index_in_dim(mixing, freq_index, 1, keepdims=False)
    every_pred = lax.all_gather(rows_pred[None], "freq", axis=0, tiled=True)
    residual_rows = (
        jnp.einsum("g,grs->rs", weights_row, every_pred, precision=lax.Precision.HIGHEST)
        - rows_data
    )
    every_res = lax.all_gather(residual_rows[None], "freq", axis=0, tiled=True)
    adjoint_rows = jnp.einsum("g,grs->rs", weights_col, every_res, precision=lax.Precision.HIGHEST)
    return (residual_rows, adjoint_rows)


def body(model_in, observed, right_factors, left_factors, tile_map, tile_ranks, window_mix):
    tile_index = lax.axis_index("tiles")
    parity = tile_index % 2
    tile_count = lax.axis_size("tiles")
    tile_rows = tile_count // 2
    per_device = tile_map.shape[1]
    freq_index = lax.axis_index("freq")
    right_local = right_factors[0, 0]
    left_local = left_factors[0, 0]
    rank_width = right_local.shape[2] // 2
    half_rows = model_in.shape[1]
    width_cols = model_in.shape[2]
    keep_rows = rank_mask(tile_ranks[0, 0], rank_width)
    column_half = tile_index // 2 // per_device
    own_model = model_in[0]
    other_model = from_partner(own_model, "tiles", 0)
    column_block = ordered(parity, own_model, other_model)
    coeffs = jnp.where(keep_rows, conjugate_apply(right_local, column_block), 0.0).astype(
        jnp.bfloat16
    )
    targets = 2 * tile_map[0] + column_half
    outgoing = jnp.zeros((tile_count, rank_width, width_cols), jnp.bfloat16).at[targets].set(coeffs)
    incoming = lax.all_to_all(outgoing, "tiles", split_axis=0, concat_axis=0, tiled=True)
    paired = incoming.reshape(tile_rows, 2, rank_width, width_cols)
    merged = paired[:, 0] + paired[:, 1]
    row_coeffs = lax.dynamic_slice_in_dim(merged, parity * per_device, per_device, 0)
    partial_value = factor_apply(left_local, row_coeffs)
    own_data = observed[0].astype(jnp.float32)
    given_rows = lax.dynamic_slice_in_dim(partial_value, (1 - parity) * half_rows, half_rows, 0)
    received = from_partner(given_rows, "tiles", 0)
    own_pred = lax.dynamic_slice_in_dim(partial_value, parity * half_rows, half_rows, 0) + received
    residual, own_adjoint = window_step(window_mix, freq_index, own_pred, own_data)
    own_bf = own_adjoint.astype(jnp.bfloat16)
    other_bf = from_partner(own_bf, "tiles", 0)
    adjoint_block = ordered(parity, own_bf, other_bf)
    back_coeffs = conjugate_apply(left_local, adjoint_block).astype(jnp.bfloat16)
    doubled = jnp.repeat(back_coeffs, 2, axis=0)
    empty_slots = jnp.zeros((tile_count, rank_width, width_cols), jnp.bfloat16)
    outgoing_back = lax.dynamic_update_slice_in_dim(
        empty_slots, doubled, parity * 2 * per_device, 0
    )
    returned = lax.all_to_all(outgoing_back, "tiles", split_axis=0, concat_axis=0, tiled=True)
    by_row = lax.dynamic_index_in_dim(
        returned.reshape(tile_rows, 2, rank_width, width_cols), column_half, 1, keepdims=False
    )
    picked = jnp.where(keep_rows, by_row[tile_map[0]], 0.0)
    grad_partial = factor_apply(right_local, picked)
    given_grad = lax.dynamic_slice_in_dim(grad_partial, (1 - parity) * half_rows, half_rows, 0)
    received_grad = from_partner(given_grad, "tiles", 0)
    gradient = (
        lax.dynamic_slice_in_dim(grad_partial, parity * half_rows, half_rows, 0) + received_grad
    )
    return (residual[None], gradient[None])


def solution(mesh):
    placed = (
        P("freq", "tiles", None),
        P("freq", "tiles", None),
        P("freq", "tiles", None, None, None),
        P("freq", "tiles", None, None, None),
        P("tiles", None),
        P("freq", "tiles", None),
        P(),
    )
    return jax.shard_map(
        body,
        mesh=mesh,
        in_specs=placed,
        out_specs=(P("freq", "tiles", None), P("freq", "tiles", None)),
        check_vma=False,
    )
```

profile of v0, /device:TPU:0, one launch (start us, length us, event | category | flops | bytes accessed | tf_op | source)
XLA Modules:
  0.0 64.4 jit_solution(17432492704546929525)
XLA Ops:
  0.6 0.0 copy-start
  0.6 3.0 %collective-permute-start = (bf16[128,128]{1,0:T(8,128)(2,1)}, bf16[128,128]{1,0:T(8,128)(2,1)S(1)}, u32[]{:S(2)}, u32[]{:S(2)}) collective-permute-start(bf16[128,128]{1,0:T(8,128)(2,1)} %bitcast.89), channel_id=1, source_target_pairs={{0,4},{4,0},{8,12},{12,8},{16,20},{20,16},{24,28},{28,24},{1,5},{5... | collective-permute-start | bytes 98312 | tf_op jit(solution)/shard_map/ppermute | solution.py:10
  3.7 0.0 copy-start.5
  3.7 0.7 %copy-done.5 = s32[1,2]{1,0:T(1,128)S(1)} copy-done((s32[1,2]{1,0:T(1,128)S(1)}, s32[1,2]{1,0:T(1,128)}, u32[]{:S(2)}) %copy-start.5) | copy-done | bytes 32
  4.3 0.0 copy-start.7
  4.3 0.7 %copy-done.7 = s32[1,1,2]{2,1,0:T(1,128)S(1)} copy-done((s32[1,1,2]{2,1,0:T(1,128)S(1)}, s32[1,1,2]{2,1,0:T(1,128)}, u32[]{:S(2)}) %copy-start.7) | copy-done | bytes 32
  5.0 0.1 iota_compare_fusion
  5.1 0.0 copy-start.6
  5.1 1.0 %copy.13 = bf16[2,256,128]{1,2,0:T(8,128)(2,1)S(1)} copy(bf16[2,256,128]{2,1,0:T(8,128)(2,1)} %bitcast.82) | data formatting | bytes 262144 | tf_op jit(solution)/shard_map/squeeze | solution.py:63
  6.1 0.0 collective-permute-done
  6.1 0.0 copy-done.6
  6.1 0.2 fusion.4
  6.3 0.1 slice_add_fusion.1
  6.4 0.1 fusion.10
  6.5 0.7 %broadcast.73.clone = bf16[8,64,128]{2,1,0:T(8,128)(2,1)} broadcast(bf16[]{:T(256)} %constant.63.clone.1), dimensions={} | broadcast | bytes 131074 | tf_op jit(solution)/shard_map/broadcast.8
  7.2 1.9 %scatter_fusion = bf16[8,64,128]{2,1,0:T(8,128)(2,1)} fusion(bf16[8,64,128]{2,1,0:T(8,128)(2,1)} %broadcast.73.clone, s32[2]{0:T(128)S(1)} %get-tuple-element.17, bf16[2,64,128]{2,1,0:T(8,128)(2,1)S(1)} %fusion.10), kind=kCustom, calls=%fused_computation.1 | custom fusion | bytes 98312 | tf_op jit(solution)/shard_map/scatter | solution.py:77
  9.1 6.0 %all-to-all-start = ((bf16[8,64,128]{2,1,0:T(8,128)(2,1)}), bf16[8,64,128]{2,1,0:T(8,128)(2,1)S(1)}, u32[]{:S(2)}, u32[]{:S(2)}) async-start(bf16[8,64,128]{2,1,0:T(8,128)(2,1)} %scatter_fusion), calls=%async_computation | async-start | bytes 262144 | tf_op jit(solution)/shard_map/all_to_all | solution.py:78
  15.1 7.3 %all-to-all-done = bf16[8,64,128]{2,1,0:T(8,128)(2,1)S(1)} async-done(((bf16[8,64,128]{2,1,0:T(8,128)(2,1)}), bf16[8,64,128]{2,1,0:T(8,128)(2,1)S(1)}, u32[]{:S(2)}, u32[]{:S(2)}) %all-to-all-start) | async-done | bytes 131104 | tf_op jit(solution)/shard_map/all_to_all | solution.py:78
  22.5 0.0 copy-start.1
  22.5 0.1 copy.14
  22.6 0.8 %copy-done.1 = bf16[1,1,2,256,128]{4,3,2,1,0:T(8,128)(2,1)S(1)} copy-done((bf16[1,1,2,256,128]{4,3,2,1,0:T(8,128)(2,1)S(1)}, bf16[1,1,2,256,128]{4,3,2,1,0:T(8,128)(2,1)}, u32[]{:S(2)}) %copy-start.1) | copy-done | bytes 131096
  23.4 0.2 convolution_bitcast_fusion.1
  23.6 0.3 collective-permute-start.1
  23.9 0.0 copy-done
  23.9 0.2 fusion.30
  24.1 3.9 %collective-permute-done.1 = f32[128,128]{0,1:T(8,128)S(1)} collective-permute-done((f32[128,128]{0,1:T(8,128)S(1)}, f32[128,128]{0,1:T(8,128)S(1)}, u32[]{:S(2)}, u32[]{:S(2)}) %collective-permute-start.1) | collective-permute-done | bytes 65568 | tf_op jit(solution)/shard_map/ppermute | solution.py:10
  27.9 5.8 %all-gather = f32[512,128]{0,1:T(8,128)S(1)} all-gather(f32[128,128]{0,1:T(8,128)S(1)} %bitcast_add_fusion.1), channel_id=2, replica_groups=mesh['tiles'=8,'freq'=4] {'freq'}, dimensions={0}, use_global_device_ids=true | all-gather | bytes 327680 | tf_op jit(solution)/shard_map/all_gather | solution.py:46
  33.7 0.1 reshape.112
  33.8 0.6 fusion.32
  34.4 0.0 copy-start.4
  34.4 0.1 copy.18
  34.5 0.7 %copy-done.4 = bf16[1,128,128]{2,1,0:T(8,128)(2,1)S(1)} copy-done((bf16[1,128,128]{2,1,0:T(8,128)(2,1)S(1)}, bf16[1,128,128]{2,1,0:T(8,128)(2,1)}, u32[]{:S(2)}) %copy-start.4) | copy-done | bytes 32792
  35.2 0.0 copy-start.3
  35.2 5.9 %all-gather.1 = f32[512,128]{1,0:T(8,128)S(1)} all-gather(f32[128,128]{1,0:T(8,128)S(1)} %convert_subtract_fusion), channel_id=3, replica_groups=mesh['tiles'=8,'freq'=4] {'freq'}, dimensions={0}, use_global_device_ids=true | all-gather | bytes 327680 | tf_op jit(solution)/shard_map/all_gather | solution.py:51
  41.0 0.0 copy-done.3
  41.1 0.7 %fusion = f32[1,128,128]{2,0,1:T(1,128)S(1)} fusion(f32[4,128,128]{2,1,0:T(8,128)S(1)} %bitcast.75, f32[4]{0:T(128)S(1)} %fusion.30), kind=kOutput, calls=%fused_computation.4 | convolution fusion | flops 786432 | bytes 327696 | tf_op jit(solution)/shard_map/g,grs->rs/dot_general | solution.py:52
  41.8 0.3 collective-permute-start.2
  42.0 0.1 copy.15
  42.2 3.6 %collective-permute-done.2 = bf16[128,128]{1,0:T(8,128)(2,1)S(1)} collective-permute-done((bf16[128,128]{1,0:T(8,128)(2,1)S(1)}, bf16[128,128]{1,0:T(8,128)(2,1)S(1)}, u32[]{:S(2)}, u32[]{:S(2)}) %collective-permute-start.2) | collective-permute-done | bytes 32800 | tf_op jit(solution)/shard_map/ppermute | solution.py:10
  45.7 0.2 fusion.16
  45.9 0.1 fusion.3
  46.0 0.1 pad_maximum_fusion
  46.1 0.7 %broadcast.73 = bf16[8,64,128]{2,1,0:T(8,128)(2,1)} broadcast(bf16[]{:T(256)} %constant.63.clone.1), dimensions={} | broadcast | bytes 131074 | tf_op jit(solution)/shard_map/broadcast.8
  46.8 0.6 constant_dynamic-update-slice_fusion
  47.4 3.4 %all-to-all-start.1 = ((bf16[8,64,128]{2,1,0:T(8,128)(2,1)}), bf16[8,64,128]{2,1,0:T(8,128)(2,1)S(1)}, u32[]{:S(2)}, u32[]{:S(2)}) async-start(bf16[8,64,128]{2,1,0:T(8,128)(2,1)} %constant_dynamic-update-slice_fusion), calls=%async_computation.1 | async-start | bytes 262144 | tf_op jit(solution)/shard_map/all_to_all | solution.py:97
  50.8 7.3 %all-to-all-done.1 = bf16[8,64,128]{2,1,0:T(8,128)(2,1)S(1)} async-done(((bf16[8,64,128]{2,1,0:T(8,128)(2,1)}), bf16[8,64,128]{2,1,0:T(8,128)(2,1)S(1)}, u32[]{:S(2)}, u32[]{:S(2)}) %all-to-all-start.1) | async-done | bytes 131104 | tf_op jit(solution)/shard_map/all_to_all | solution.py:97
  58.1 0.0 copy-start.2
  58.1 0.6 gather_fusion
  58.7 0.1 broadcast_select_fusion
  58.8 0.1 slice_negate_fusion
  58.8 0.2 copy-done.2
  59.0 0.3 convolution_bitcast_fusion
  59.3 0.3 collective-permute-start.3
  59.6 4.1 %collective-permute-done.3 = f32[128,128]{0,1:T(8,128)S(1)} collective-permute-done((f32[128,128]{0,1:T(8,128)S(1)}, f32[128,128]{0,1:T(8,128)S(1)}, u32[]{:S(2)}, u32[]{:S(2)}) %collective-permute-start.3) | collective-permute-done | bytes 65568 | tf_op jit(solution)/shard_map/ppermute | solution.py:10
  63.6 0.7 %copy.17 = f32[1,128,128]{2,1,0:T(8,128)} copy(f32[1,128,128]{1,2,0:T(8,128)S(1)} %fusion.27) | data formatting | bytes 131072
  (13 shorter events, 0.1 us)
Async XLA Ops:
  0.6 23.2 %copy-start = (f32[4,4]{1,0:T(4,128)S(1)}, f32[4,4]{1,0:T(4,128)}, u32[]{:S(2)}) copy-start(f32[4,4]{1,0:T(4,128)} %param.13) | copy-start | bytes 196
  0.6 5.4 %collective-permute-start = (bf16[128,128]{1,0:T(8,128)(2,1)}, bf16[128,128]{1,0:T(8,128)(2,1)S(1)}, u32[]{:S(2)}, u32[]{:S(2)}) collective-permute-start(bf16[128,128]{1,0:T(8,128)(2,1)} %bitcast.89), channel_id=1, source_target_pairs={{0,4},{4,0},{8,12},{12,8},{16,20},{20,16},{24,28},{28,24},{1,5},{5... | collective-permute-start | bytes 98312 | tf_op jit(solution)/shard_map/ppermute | solution.py:10
  3.7 0.7 %copy-start.5 = (s32[1,2]{1,0:T(1,128)S(1)}, s32[1,2]{1,0:T(1,128)}, u32[]{:S(2)}) copy-start(s32[1,2]{1,0:T(1,128)} %param.11) | copy-start | bytes 28
  4.3 0.7 %copy-start.7 = (s32[1,1,2]{2,1,0:T(1,128)S(1)}, s32[1,1,2]{2,1,0:T(1,128)}, u32[]{:S(2)}) copy-start(s32[1,1,2]{2,1,0:T(1,128)} %param.12) | copy-start | bytes 28
  5.1 1.0 %copy-start.6 = (bf16[1,128,128]{2,1,0:T(8,128)(2,1)S(1)}, bf16[1,128,128]{2,1,0:T(8,128)(2,1)}, u32[]{:S(2)}) copy-start(bf16[1,128,128]{2,1,0:T(8,128)(2,1)} %param.7) | copy-start | bytes 98308
  9.1 13.4 %all-to-all-start = ((bf16[8,64,128]{2,1,0:T(8,128)(2,1)}), bf16[8,64,128]{2,1,0:T(8,128)(2,1)S(1)}, u32[]{:S(2)}, u32[]{:S(2)}) async-start(bf16[8,64,128]{2,1,0:T(8,128)(2,1)} %scatter_fusion), calls=%async_computation | async-start | bytes 262144 | tf_op jit(solution)/shard_map/all_to_all | solution.py:78
  22.5 0.9 %copy-start.1 = (bf16[1,1,2,256,128]{4,3,2,1,0:T(8,128)(2,1)S(1)}, bf16[1,1,2,256,128]{4,3,2,1,0:T(8,128)(2,1)}, u32[]{:S(2)}) copy-start(bf16[1,1,2,256,128]{4,3,2,1,0:T(8,128)(2,1)} %param.10) | copy-start | bytes 393220
  23.6 4.3 %collective-permute-start.1 = (f32[128,128]{0,1:T(8,128)S(1)}, f32[128,128]{0,1:T(8,128)S(1)}, u32[]{:S(2)}, u32[]{:S(2)}) collective-permute-start(f32[128,128]{0,1:T(8,128)S(1)} %dynamic-slice_bitcast_fusion.2), channel_id=1, source_target_pairs={{0,4},{4,0},{8,12},{12,8},{16,20},{20,16},{24,28},{28,24},{1,5},{5... | collective-permute-start | bytes 196616 | tf_op jit(solution)/shard_map/ppermute | solution.py:10
  34.4 0.8 %copy-start.4 = (bf16[1,128,128]{2,1,0:T(8,128)(2,1)S(1)}, bf16[1,128,128]{2,1,0:T(8,128)(2,1)}, u32[]{:S(2)}) copy-start(bf16[1,128,128]{2,1,0:T(8,128)(2,1)} %param.8) | copy-start | bytes 98308
  35.2 5.9 %copy-start.3 = (f32[128,128]{1,0:T(8,128)}, f32[128,128]{1,0:T(8,128)S(1)}, u32[]{:S(2)}) copy-start(f32[128,128]{1,0:T(8,128)S(1)} %convert_subtract_fusion) | copy-start | bytes 196612
  41.8 4.0 %collective-permute-start.2 = (bf16[128,128]{1,0:T(8,128)(2,1)S(1)}, bf16[128,128]{1,0:T(8,128)(2,1)S(1)}, u32[]{:S(2)}, u32[]{:S(2)}) collective-permute-start(bf16[128,128]{1,0:T(8,128)(2,1)S(1)} %convert_element_type.18), channel_id=1, source_target_pairs={{0,4},{4,0},{8,12},{12,8},{16,20},{20,16},{24,28},{28,24},{1,5},{5... | collective-permute-start | bytes 98312 | tf_op jit(solution)/shard_map/ppermute | solution.py:10
  47.4 10.7 %all-to-all-start.1 = ((bf16[8,64,128]{2,1,0:T(8,128)(2,1)}), bf16[8,64,128]{2,1,0:T(8,128)(2,1)S(1)}, u32[]{:S(2)}, u32[]{:S(2)}) async-start(bf16[8,64,128]{2,1,0:T(8,128)(2,1)} %constant_dynamic-update-slice_fusion), calls=%async_computation.1 | async-start | bytes 262144 | tf_op jit(solution)/shard_map/all_to_all | solution.py:97
  58.1 0.9 %copy-start.2 = (bf16[1,1,2,256,128]{4,3,2,1,0:T(8,128)(2,1)S(1)}, bf16[1,1,2,256,128]{4,3,2,1,0:T(8,128)(2,1)}, u32[]{:S(2)}) copy-start(bf16[1,1,2,256,128]{4,3,2,1,0:T(8,128)(2,1)} %param.9) | copy-start | bytes 393220
  59.3 4.3 %collective-permute-start.3 = (f32[128,128]{0,1:T(8,128)S(1)}, f32[128,128]{0,1:T(8,128)S(1)}, u32[]{:S(2)}, u32[]{:S(2)}) collective-permute-start(f32[128,128]{0,1:T(8,128)S(1)} %dynamic-slice_bitcast_fusion), channel_id=1, source_target_pairs={{0,4},{4,0},{8,12},{12,8},{16,20},{20,16},{24,28},{28,24},{1,5},{5... | collective-permute-start | bytes 196616 | tf_op jit(solution)/shard_map/ppermute | solution.py:10
where the time goes:
time: 65 us; the launch traced here: 64.4 us
  waiting for transfers between devices  26.1 us (40%)
  starting transfers between devices  13.2 us (20%)
  blocking collectives  11.7 us (18%)
  local copies, waits for them, and re-layouts  9.71 us (15%)
  matrix products  2.07 us (3%)
  between operations  0.89 us (1%)
  other arithmetic  0.69 us (1%)
    ppermute x4, waiting for transfers between devices, from_partner(): return lax.ppermute(value, axis, pairs)  11.5 us
    all_to_all x1, waiting for transfers between devices, body(): lax.all_to_all(outgoing, 'tiles', split_axis=0, concat_axis=0, tiled=True)  7.34 us
    all_to_all x1, waiting for transfers between devices, body(): lax.all_to_all(outgoing_back, 'tiles', split_axis=0, concat_axis=0, tiled...  7.26 us
    all_to_all x1, starting transfers between devices, body(): lax.all_to_all(outgoing, 'tiles', split_axis=0, concat_axis=0, tiled=True)  6.01 us
    all_gather x1, blocking collectives, window_step(): every_res = lax.all_gather(residual_rows[None], 'freq', axis=0, tiled=True)  5.87 us
    all_gather x1, blocking collectives, window_step(): every_pred = lax.all_gather(rows_pred[None], 'freq', axis=0, tiled=True)  5.79 us
    ppermute x4, starting transfers between devices, from_partner(): return lax.ppermute(value, axis, pairs)  3.86 us
    unnamed x17, local copies, waits for them, and re-layouts  3.63 us
  transfers between devices with their start and end apart: 6, of which 5 were waited for; matrix products, arithmetic and copies ran while one was open for 2% of the time, Pallas kernels for 0%

commit v1 on v0

--- a/solution.py
+++ b/solution.py
@@ -2,6 +2,22 @@
 import jax.numpy as jnp
 from jax import lax
 from jax.sharding import PartitionSpec as P
+
+
+def ring_product(x, axis, dim, contribution):
+    size, index, rows = (lax.axis_size(axis), lax.axis_index(axis), x.shape[dim])
+    forward = [(i, (i + 1) % size) for i in range(size)]
+    behind = [(i, (i - 1) % size) for i in range(size)]
+    middle = size // 2
+    from_left = from_right = x
+    so_far = contribution(x, index * rows)
+    for turn in range(1, middle + 1):
+        from_left = lax.ppermute(from_left, axis, forward)
+        if turn < size - middle:
+            from_right = lax.ppermute(from_right, axis, behind)
+            so_far = so_far + contribution(from_right, (index + turn) % size * rows)
+        so_far = so_far + contribution(from_left, (index - turn) % size * rows)
+    return so_far
 
 
 def from_partner(value, axis, apart):
@@ -43,9 +59,18 @@
 def window_step(mixing, freq_index, rows_pred, rows_data):
     weights_row = lax.dynamic_index_in_dim(mixing, freq_index, 0, keepdims=False)
     weights_col = lax.dynamic_index_in_dim(mixing, freq_index, 1, keepdims=False)
-    every_pred = lax.all_gather(rows_pred[None], "freq", axis=0, tiled=True)
     residual_rows = (
-        jnp.einsum("g,grs->rs", weights_row, every_pred, precision=lax.Precision.HIGHEST)
+        ring_product(
+            rows_pred[None],
+            "freq",
+            0,
+            lambda own_block, start: jnp.einsum(
+                "g,grs->rs",
+                lax.dynamic_slice_in_dim(weights_row, start, own_block.shape[0], axis=0),
+                own_block,
+                precision=lax.Precision.HIGHEST,
+            ),
+        )
         - rows_data
     )
     every_res = lax.all_gather(residual_rows[None], "freq", axis=0, tiled=True)

time: 65 us -> 67.6 us (1.040)
  blocking collectives: 11.7 us -> 5.79 us
  waiting for transfers between devices: 26.1 us -> 29 us
  other arithmetic: 0.69 us -> 3.18 us
  local copies, waits for them, and re-layouts: 9.71 us -> 11.8 us
  starting transfers between devices: 13.2 us -> 15 us
  matrix products: 2.07 us -> 1.37 us
    all_gather x1 -> x0, blocking collectives: 5.79 us -> none  [window_step(): every_pred = lax.all_gather(rows_pred[None], 'freq', axis=0, tiled=True)]
    ppermute x0 -> x3, waiting for transfers between devices: none -> 3.4 us  [the longest x2 3.39 us: ring_product(): from_left = lax.ppermute(from_left, axis, forward)]
    sub x1, other arithmetic: 0.01 us -> 2.5 us  [window_step(): ring_product(rows_pred[None], 'freq', 0, lambda own_block, start: jnp.ein...]
    ppermute x0 -> x3, starting transfers between devices: none -> 1.79 us  [the longest x1 1.73 us: ring_product(): from_right = lax.ppermute(from_right, axis, behind)]
    unnamed x17, local copies, waits for them, and re-layouts: 3.63 us -> 5.12 us
  transfers between devices with their start and end apart: 6 -> 9, of which waited for: 5 -> 7; matrix products, arithmetic and copies ran while one was open for 2% -> 4% of each run, Pallas kernels for 0% -> 0%
where the time goes in v1:
time: 67.6 us; the launch traced here: 67 us
  waiting for transfers between devices  29 us (43%)
  starting transfers between devices  15 us (22%)
  local copies, waits for them, and re-layouts  11.8 us (17%)
  blocking collectives  5.79 us (9%)
  other arithmetic  3.18 us (5%)
  matrix products  1.37 us (2%)
  between operations  0.87 us (1%)
    ppermute x4, waiting for transfers between devices, from_partner(): return lax.ppermute(value, axis, pairs)  11 us
    all_to_all x1, waiting for transfers between devices, body(): lax.all_to_all(outgoing, 'tiles', split_axis=0, concat_axis=0, tiled=True)  7.34 us
    all_to_all x1, waiting for transfers between devices, body(): lax.all_to_all(outgoing_back, 'tiles', split_axis=0, concat_axis=0, tiled...  7.26 us
    all_to_all x1, starting transfers between devices, body(): lax.all_to_all(outgoing, 'tiles', split_axis=0, concat_axis=0, tiled=True)  6.02 us
    all_gather x1, blocking collectives, window_step(): every_res = lax.all_gather(residual_rows[None], 'freq', axis=0, tiled=True)  5.79 us
    unnamed x17, local copies, waits for them, and re-layouts  5.12 us
    ppermute x4, starting transfers between devices, from_partner(): return lax.ppermute(value, axis, pairs)  3.87 us
    ppermute x2, waiting for transfers between devices, ring_product(): from_left = lax.ppermute(from_left, axis, forward)  3.39 us
  transfers between devices with their start and end apart: 9, of which 7 were waited for; matrix products, arithmetic and copies ran while one was open for 4% of the time, Pallas kernels for 0%

profile of v1, /device:TPU:0, one launch (start us, length us, event | category | flops | bytes accessed | tf_op | source)
XLA Modules:
  0.0 67.0 jit_solution(16591217300064009832)
XLA Ops:
  0.6 3.0 %collective-permute-start = (bf16[128,128]{1,0:T(8,128)(2,1)}, bf16[128,128]{1,0:T(8,128)(2,1)S(1)}, u32[]{:S(2)}, u32[]{:S(2)}) collective-permute-start(bf16[128,128]{1,0:T(8,128)(2,1)} %bitcast.104), channel_id=1, source_target_pairs={{0,4},{4,0},{8,12},{12,8},{16,20},{20,16},{24,28},{28,24},{1,5},{5... | collective-permute-start | bytes 98312 | tf_op jit(solution)/shard_map/ppermute | solution.py:26
  3.7 0.0 copy-start.4
  3.7 0.7 copy-done.4
  4.3 0.0 copy-start.6
  4.3 0.7 copy-done.6
  5.0 0.1 iota_compare_fusion
  5.1 0.0 copy-start.5
  5.1 1.0 %copy.15 = bf16[2,256,128]{1,2,0:T(8,128)(2,1)S(1)} copy(bf16[2,256,128]{2,1,0:T(8,128)(2,1)} %bitcast.97) | data formatting | bytes 262144 | tf_op jit(solution)/shard_map/squeeze | solution.py:88
  6.1 0.0 collective-permute-done
  6.1 0.0 copy-done.5
  6.1 0.2 fusion.2
  6.3 0.1 slice_add_fusion.1
  6.4 0.1 fusion.8
  6.5 0.7 broadcast.86.clone
  7.2 1.9 %scatter_fusion = bf16[8,64,128]{2,1,0:T(8,128)(2,1)} fusion(bf16[8,64,128]{2,1,0:T(8,128)(2,1)} %broadcast.86.clone, s32[2]{0:T(128)S(1)} %get-tuple-element.21, bf16[2,64,128]{2,1,0:T(8,128)(2,1)S(1)} %fusion.8), kind=kCustom, calls=%fused_computation.1 | custom fusion | bytes 98312 | tf_op jit(solution)/shard_map/scatter | solution.py:102
  9.0 6.0 %all-to-all-start = ((bf16[8,64,128]{2,1,0:T(8,128)(2,1)}), bf16[8,64,128]{2,1,0:T(8,128)(2,1)S(1)}, u32[]{:S(2)}, u32[]{:S(2)}) async-start(bf16[8,64,128]{2,1,0:T(8,128)(2,1)} %scatter_fusion), calls=%async_computation | async-start | bytes 262144 | tf_op jit(solution)/shard_map/all_to_all | solution.py:103
  15.1 7.3 %all-to-all-done = bf16[8,64,128]{2,1,0:T(8,128)(2,1)S(1)} async-done(((bf16[8,64,128]{2,1,0:T(8,128)(2,1)}), bf16[8,64,128]{2,1,0:T(8,128)(2,1)S(1)}, u32[]{:S(2)}, u32[]{:S(2)}) %all-to-all-start) | async-done | bytes 131104 | tf_op jit(solution)/shard_map/all_to_all | solution.py:103
  22.4 0.0 copy-start
  22.5 0.1 copy.16
  22.6 0.8 %copy-done = bf16[1,1,2,256,128]{4,3,2,1,0:T(8,128)(2,1)S(1)} copy-done((bf16[1,1,2,256,128]{4,3,2,1,0:T(8,128)(2,1)S(1)}, bf16[1,1,2,256,128]{4,3,2,1,0:T(8,128)(2,1)}, u32[]{:S(2)}) %copy-start) | copy-done | bytes 131096
  23.4 0.2 convolution_bitcast_fusion.1
  23.6 0.3 collective-permute-start.1
  23.9 4.1 %collective-permute-done.1 = f32[128,128]{0,1:T(8,128)S(1)} collective-permute-done((f32[128,128]{0,1:T(8,128)S(1)}, f32[128,128]{0,1:T(8,128)S(1)}, u32[]{:S(2)}, u32[]{:S(2)}) %collective-permute-start.1) | collective-permute-done | bytes 65568 | tf_op jit(solution)/shard_map/ppermute | solution.py:26
  27.9 0.1 collective-permute-start.3
  28.0 1.7 %collective-permute-start.2 = (f32[1,128,128]{1,2,0:T(8,128)S(1)}, f32[1,128,128]{1,2,0:T(8,128)S(1)}, u32[]{:S(2)}, u32[]{:S(2)}) collective-permute-start(f32[1,128,128]{1,2,0:T(8,128)S(1)} %fusion.28), channel_id=1, source_target_pairs={{0,3},{1,0},{2,1},{3,2},{4,7},{5,4},{6,5},{7,6},{8,11},{9,8},{10,9... | collective-permute-start | bytes 196616 | tf_op jit(solution)/shard_map/ppermute | solution.py:17
  29.7 1.9 %collective-permute-done.3 = f32[1,128,128]{1,2,0:T(8,128)S(1)} collective-permute-done((f32[1,128,128]{1,2,0:T(8,128)S(1)}, f32[1,128,128]{1,2,0:T(8,128)S(1)}, u32[]{:S(2)}, u32[]{:S(2)}) %collective-permute-start.3) | collective-permute-done | bytes 65568 | tf_op jit(solution)/shard_map/ppermute | solution.py:15
  31.7 0.0 collective-permute-start.4
  31.7 0.0 copy-start.2
  31.7 0.8 %copy-done.2 = bf16[1,128,128]{2,1,0:T(8,128)(2,1)S(1)} copy-done((bf16[1,128,128]{2,1,0:T(8,128)(2,1)S(1)}, bf16[1,128,128]{2,1,0:T(8,128)(2,1)}, u32[]{:S(2)}) %copy-start.2) | copy-done | bytes 32792
  32.4 0.0 copy-start.3
  32.4 0.1 copy.17
  32.5 0.6 copy-done.3
  33.1 0.2 fusion.29
  33.3 0.6 fusion.42
  33.9 0.0 collective-permute-done.2
  33.9 1.5 %collective-permute-done.4 = f32[1,128,128]{1,2,0:T(8,128)S(1)} collective-permute-done((f32[1,128,128]{1,2,0:T(8,128)S(1)}, f32[1,128,128]{1,2,0:T(8,128)S(1)}, u32[]{:S(2)}, u32[]{:S(2)}) %collective-permute-start.4) | collective-permute-done | bytes 65568 | tf_op jit(solution)/shard_map/ppermute | solution.py:15
  35.4 2.5 %convert_subtract_fusion = f32[128,128]{0,1:T(8,128)S(1)} fusion(f32[1,128,128]{1,2,0:T(8,128)S(1)} %collective-permute-done.4, f32[1,128,128]{1,2,0:T(8,128)S(1)} %collective-permute-done.3, f32[1,128,128]{1,2,0:T(8,128)S(1)} %collective-permute-done.2, bf16[1,128,128]{1,2,0:T(8,128)(2,1)S(1)} %copy.17, f32[]{:T(128)} %bitcast.22, f32[]{:T(128)} %bitcast.20, ...), kind=kLoop, calls=%fused_computation.36 | loop fusion | flops 163840 | bytes 426004 | tf_op jit(solution)/shard_map/sub | solution.py:63
  37.9 5.8 %all-gather = f32[512,128]{0,1:T(8,128)S(1)} all-gather(f32[128,128]{0,1:T(8,128)S(1)} %convert_subtract_fusion), channel_id=2, replica_groups=mesh['tiles'=8,'freq'=4] {'freq'}, dimensions={0}, use_global_device_ids=true | all-gather | bytes 327680 | tf_op jit(solution)/shard_map/all_gather | solution.py:76
  43.7 0.1 reshape.147
  43.8 0.6 fusion.32
  44.3 0.1 copy.22
  44.4 0.3 collective-permute-start.5
  44.7 0.1 copy.18
  44.9 3.6 %collective-permute-done.5 = bf16[128,128]{1,0:T(8,128)(2,1)S(1)} collective-permute-done((bf16[128,128]{1,0:T(8,128)(2,1)S(1)}, bf16[128,128]{1,0:T(8,128)(2,1)S(1)}, u32[]{:S(2)}, u32[]{:S(2)}) %collective-permute-start.5) | collective-permute-done | bytes 32800 | tf_op jit(solution)/shard_map/ppermute | solution.py:26
  48.4 0.2 fusion.14
  48.6 0.1 fusion.1
  48.7 0.1 pad_maximum_fusion
  48.8 0.7 broadcast.86
  49.5 0.6 constant_dynamic-update-slice_fusion
  50.1 3.4 %all-to-all-start.1 = ((bf16[8,64,128]{2,1,0:T(8,128)(2,1)}), bf16[8,64,128]{2,1,0:T(8,128)(2,1)S(1)}, u32[]{:S(2)}, u32[]{:S(2)}) async-start(bf16[8,64,128]{2,1,0:T(8,128)(2,1)} %constant_dynamic-update-slice_fusion), calls=%async_computation.1 | async-start | bytes 262144 | tf_op jit(solution)/shard_map/all_to_all | solution.py:122
  53.5 7.3 %all-to-all-done.1 = bf16[8,64,128]{2,1,0:T(8,128)(2,1)S(1)} async-done(((bf16[8,64,128]{2,1,0:T(8,128)(2,1)}), bf16[8,64,128]{2,1,0:T(8,128)(2,1)S(1)}, u32[]{:S(2)}, u32[]{:S(2)}) %all-to-all-start.1) | async-done | bytes 131104 | tf_op jit(solution)/shard_map/all_to_all | solution.py:122
  60.8 0.0 copy-start.1
  60.8 0.6 gather_fusion
  61.3 0.1 broadcast_select_fusion
  61.4 0.1 slice_negate_fusion
  61.5 0.2 copy-done.1
  61.7 0.3 convolution_bitcast_fusion
  61.9 0.3 collective-permute-start.6
  62.2 0.7 %copy.20 = f32[1,128,128]{2,1,0:T(8,128)} copy(f32[1,128,128]{1,2,0:T(8,128)S(1)} %bitcast.90) | data formatting | bytes 131072
  63.0 3.3 %collective-permute-done.6 = f32[128,128]{0,1:T(8,128)S(1)} collective-permute-done((f32[128,128]{0,1:T(8,128)S(1)}, f32[128,128]{0,1:T(8,128)S(1)}, u32[]{:S(2)}, u32[]{:S(2)}) %collective-permute-start.6) | collective-permute-done | bytes 65568 | tf_op jit(solution)/shard_map/ppermute | solution.py:26
  66.3 0.7 %copy.21 = f32[1,128,128]{2,1,0:T(8,128)} copy(f32[1,128,128]{1,2,0:T(8,128)S(1)} %fusion.25) | data formatting | bytes 131072
  (11 shorter events, 0.1 us)
Async XLA Ops:
  0.6 5.4 %collective-permute-start = (bf16[128,128]{1,0:T(8,128)(2,1)}, bf16[128,128]{1,0:T(8,128)(2,1)S(1)}, u32[]{:S(2)}, u32[]{:S(2)}) collective-permute-start(bf16[128,128]{1,0:T(8,128)(2,1)} %bitcast.104), channel_id=1, source_target_pairs={{0,4},{4,0},{8,12},{12,8},{16,20},{20,16},{24,28},{28,24},{1,5},{5... | collective-permute-start | bytes 98312 | tf_op jit(solution)/shard_map/ppermute | solution.py:26
  3.7 0.7 copy-start.4
  4.3 0.7 copy-start.6
  5.1 1.0 %copy-start.5 = (bf16[1,128,128]{2,1,0:T(8,128)(2,1)S(1)}, bf16[1,128,128]{2,1,0:T(8,128)(2,1)}, u32[]{:S(2)}) copy-start(bf16[1,128,128]{2,1,0:T(8,128)(2,1)} %param.7) | copy-start | bytes 98308
  9.0 13.4 %all-to-all-start = ((bf16[8,64,128]{2,1,0:T(8,128)(2,1)}), bf16[8,64,128]{2,1,0:T(8,128)(2,1)S(1)}, u32[]{:S(2)}, u32[]{:S(2)}) async-start(bf16[8,64,128]{2,1,0:T(8,128)(2,1)} %scatter_fusion), calls=%async_computation | async-start | bytes 262144 | tf_op jit(solution)/shard_map/all_to_all | solution.py:103
  22.4 0.9 %copy-start = (bf16[1,1,2,256,128]{4,3,2,1,0:T(8,128)(2,1)S(1)}, bf16[1,1,2,256,128]{4,3,2,1,0:T(8,128)(2,1)}, u32[]{:S(2)}) copy-start(bf16[1,1,2,256,128]{4,3,2,1,0:T(8,128)(2,1)} %param.10) | copy-start | bytes 393220
  23.6 4.3 %collective-permute-start.1 = (f32[128,128]{0,1:T(8,128)S(1)}, f32[128,128]{0,1:T(8,128)S(1)}, u32[]{:S(2)}, u32[]{:S(2)}) collective-permute-start(f32[128,128]{0,1:T(8,128)S(1)} %dynamic-slice_bitcast_fusion.2), channel_id=1, source_target_pairs={{0,4},{4,0},{8,12},{12,8},{16,20},{20,16},{24,28},{28,24},{1,5},{5... | collective-permute-start | bytes 196616 | tf_op jit(solution)/shard_map/ppermute | solution.py:26
  27.9 3.7 %collective-permute-start.3 = (f32[1,128,128]{1,2,0:T(8,128)S(1)}, f32[1,128,128]{1,2,0:T(8,128)S(1)}, u32[]{:S(2)}, u32[]{:S(2)}) collective-permute-start(f32[1,128,128]{1,2,0:T(8,128)S(1)} %fusion.28), channel_id=1, source_target_pairs={{0,1},{1,2},{2,3},{3,0},{4,5},{5,6},{6,7},{7,4},{8,9},{9,10},{10,1... | collective-permute-start | bytes 196616 | tf_op jit(solution)/shard_map/ppermute | solution.py:15
  28.0 5.9 %collective-permute-start.2 = (f32[1,128,128]{1,2,0:T(8,128)S(1)}, f32[1,128,128]{1,2,0:T(8,128)S(1)}, u32[]{:S(2)}, u32[]{:S(2)}) collective-permute-start(f32[1,128,128]{1,2,0:T(8,128)S(1)} %fusion.28), channel_id=1, source_target_pairs={{0,3},{1,0},{2,1},{3,2},{4,7},{5,4},{6,5},{7,6},{8,11},{9,8},{10,9... | collective-permute-start | bytes 196616 | tf_op jit(solution)/shard_map/ppermute | solution.py:17
  31.7 3.7 %collective-permute-start.4 = (f32[1,128,128]{1,2,0:T(8,128)S(1)}, f32[1,128,128]{1,2,0:T(8,128)S(1)}, u32[]{:S(2)}, u32[]{:S(2)}) collective-permute-start(f32[1,128,128]{1,2,0:T(8,128)S(1)} %collective-permute-done.3), channel_id=1, source_target_pairs={{0,1},{1,2},{2,3},{3,0},{4,5},{5,6},{6,7},{7,4},{8,9},{9,10},{10,1... | collective-permute-start | bytes 196616 | tf_op jit(solution)/shard_map/ppermute | solution.py:15
  31.7 0.8 %copy-start.2 = (bf16[1,128,128]{2,1,0:T(8,128)(2,1)S(1)}, bf16[1,128,128]{2,1,0:T(8,128)(2,1)}, u32[]{:S(2)}) copy-start(bf16[1,128,128]{2,1,0:T(8,128)(2,1)} %param.8) | copy-start | bytes 98308
  32.4 0.7 %copy-start.3 = (f32[4,4]{1,0:T(4,128)S(1)}, f32[4,4]{1,0:T(4,128)}, u32[]{:S(2)}) copy-start(f32[4,4]{1,0:T(4,128)} %param.13) | copy-start | bytes 196
  44.4 4.0 %collective-permute-start.5 = (bf16[128,128]{1,0:T(8,128)(2,1)S(1)}, bf16[128,128]{1,0:T(8,128)(2,1)S(1)}, u32[]{:S(2)}, u32[]{:S(2)}) collective-permute-start(bf16[128,128]{1,0:T(8,128)(2,1)S(1)} %bitcast.102), channel_id=1, source_target_pairs={{0,4},{4,0},{8,12},{12,8},{16,20},{20,16},{24,28},{28,24},{1,5},{5... | collective-permute-start | bytes 98312 | tf_op jit(solution)/shard_map/ppermute | solution.py:26
  50.1 10.7 %all-to-all-start.1 = ((bf16[8,64,128]{2,1,0:T(8,128)(2,1)}), bf16[8,64,128]{2,1,0:T(8,128)(2,1)S(1)}, u32[]{:S(2)}, u32[]{:S(2)}) async-start(bf16[8,64,128]{2,1,0:T(8,128)(2,1)} %constant_dynamic-update-slice_fusion), calls=%async_computation.1 | async-start | bytes 262144 | tf_op jit(solution)/shard_map/all_to_all | solution.py:122
  60.8 0.9 %copy-start.1 = (bf16[1,1,2,256,128]{4,3,2,1,0:T(8,128)(2,1)S(1)}, bf16[1,1,2,256,128]{4,3,2,1,0:T(8,128)(2,1)}, u32[]{:S(2)}) copy-start(bf16[1,1,2,256,128]{4,3,2,1,0:T(8,128)(2,1)} %param.9) | copy-start | bytes 393220
  61.9 4.3 %collective-permute-start.6 = (f32[128,128]{0,1:T(8,128)S(1)}, f32[128,128]{0,1:T(8,128)S(1)}, u32[]{:S(2)}, u32[]{:S(2)}) collective-permute-start(f32[128,128]{0,1:T(8,128)S(1)} %dynamic-slice_bitcast_fusion), channel_id=1, source_target_pairs={{0,4},{4,0},{8,12},{12,8},{16,20},{20,16},{24,28},{28,24},{1,5},{5... | collective-permute-start | bytes 196616 | tf_op jit(solution)/shard_map/ppermute | solution.py:26
